TPU v7x, 32 devices: a whole 2x2x4 slice. The times are simulated.
32 devices in a mesh: band: 4 (over y, x), img: 8 (over z, core).
Axes of the slice: x: 2, y: 2, z: 4, core: 2. Of those that a mesh axis runs over, the one named last changes fastest.
Arguments:
- images: bfloat16 [4, 128, 3328], P('band', 'img'), may hold values from -12 to 12
- references: bfloat16 [4, 32, 3328], P('band', 'img'), may hold values from -0.08 to 0.08
- noise_weight: float32 [4, 1664], P('band'), may hold values from 0.5 to 4
- masks: int32 [4, 16, 8, 49], P('band', 'img'), may hold values from 0 to 1, as said below
Outputs:
- weighted_sums: float32 [4, 32, 3328], P('band', 'img')
- weight_totals: float32 [32], P('img')
Inputs may be any that keep to these rules, and one draw needn't show every extreme that they name: `masks`: each entry is 0 or 1; translation number 49 // 2 is kept in every band, image block and orientation block.
All inputs are finite; a program needn't handle non-finite values.
Results may differ from a plain program's by a relative error of at most 0.0065.
Values may be sent and summed in bfloat16 or wider, within the bound.
No kernel may reach another device: no remote copies, remote signals or barrier semaphores. Data moves between devices by JAX's collectives and lax.ppermute only.
A program may use at most 64 MiB of HBM per device.

v0:
```python
import math
import jax
import jax.numpy as jnp
from jax import lax
from jax.sharding import PartitionSpec as P

BOX = 256
SIDE = 7
IMG_BLOCK = 8
PENALTY = 10000.0


def shift_angles(band, coef):
    index = jnp.arange(coef, dtype=jnp.int32)
    freq_x = (index * 37 + band * 11) % 257 - 128
    freq_y = (index * 61 + band * 29) % 129
    shift_ids = jnp.arange(SIDE * SIDE, dtype=jnp.int32)
    move_x = shift_ids // SIDE - SIDE // 2
    move_y = shift_ids % SIDE - SIDE // 2
    phase = (move_x[:, None] * freq_x[None, :] + move_y[:, None] * freq_y[None, :]).astype(
        jnp.float32
    )
    angle = phase * (2.0 * math.pi / BOX)
    return (jnp.cos(angle), jnp.sin(angle))


def align(pictures, cosine, sine):
    coef = cosine.shape[1]
    real = pictures[:, :coef].astype(jnp.float32)[:, None, :]
    imag = pictures[:, coef:].astype(jnp.float32)[:, None, :]
    out_real = real * cosine[None] - imag * sine[None]
    out_imag = real * sine[None] + imag * cosine[None]
    joined = jnp.concatenate([out_real, out_imag], axis=2).astype(jnp.bfloat16)
    return joined.reshape(pictures.shape[0] * cosine.shape[0], 2 * coef)


def prepare(projections, weight):
    doubled = jnp.concatenate([weight, weight])
    values = projections.astype(jnp.float32)
    weighted = (values * doubled[None, :]).astype(jnp.bfloat16)
    norms = jnp.sum(values * values * doubled[None, :], axis=1)
    return (weighted, norms)


def penalty(mask_block, img_block, orient_dev):
    blocks, owners, shift_count = mask_block.shape
    dropped = PENALTY * (1 - mask_block).astype(jnp.float32)
    dropped = jnp.transpose(dropped, (0, 2, 1))
    dropped = jnp.broadcast_to(
        dropped[:, None, :, :, None], (blocks, img_block, shift_count, owners, orient_dev)
    )
    return dropped.reshape(blocks * img_block * shift_count, owners * orient_dev)


def band_term(aligned, weighted, norms, dropped):
    cross = lax.dot_general(
        aligned, weighted, (((1,), (1,)), ((), ())), preferred_element_type=jnp.float32
    )
    return cross - 0.5 * norms[None, :] - dropped


def posterior(total, count):
    grid = total.reshape(count, -1)
    peak = jnp.max(grid, axis=1, keepdims=True)
    raised = jnp.exp(grid - peak)
    return (raised / jnp.sum(raised, axis=1, keepdims=True)).reshape(total.shape)


def combine_bands(partial_score):
    total = lax.psum(partial_score, "band")
    return total


def per_device(images, references, noise_weight, masks):
    band_index = lax.axis_index("band")
    coef = noise_weight.shape[1]
    cosine, sine = shift_angles(band_index, coef)
    weight = noise_weight[0]
    owned_refs = references[0]
    owned = owned_refs.shape[0]
    local_images = images[0]
    count = local_images.shape[0]
    aligned = align(local_images, cosine, sine)
    dropped = penalty(masks[0], IMG_BLOCK, owned)
    weighted, norms = prepare(lax.all_gather(references, "img", axis=1, tiled=True)[0], weight)
    partial_score = band_term(aligned, weighted, norms, dropped)
    score = combine_bands(partial_score)
    prob = posterior(score, count)
    post = prob.astype(jnp.bfloat16)
    totals = jnp.sum(prob, axis=0)
    sums = lax.dot_general(
        post, aligned, (((0,), (0,)), ((), ())), preferred_element_type=jnp.float32
    )
    mine_sums, mine_totals = (
        lax.psum_scatter(sums, "img", scatter_dimension=0, tiled=True),
        lax.psum_scatter(totals, "img", scatter_dimension=0, tiled=True),
    )
    return (mine_sums[None], mine_totals)


def solution(mesh):
    in_specs = (
        P("band", "img", None),
        P("band", "img", None),
        P("band", None),
        P("band", "img", None, None),
    )
    out_specs = (P("band", "img", None), P("img"))
    return jax.shard_map(
        per_device, mesh=mesh, in_specs=in_specs, out_specs=out_specs, check_vma=False
    )
```

profile of v0, /device:TPU:0, one launch (start us, length us, event | category | flops | bytes accessed | tf_op | source)
XLA Modules:
  0.0 160.8 jit_solution(395642710302518891)
XLA Ops:
  7.2 0.9 slice_convert_fusion.1
  8.1 1.4 fusion.5
  9.5 3.3 %add_convert_fusion = (bf16[16,49,1664]{2,1,0:T(8,128)(2,1)S(1)}, bf16[16,49,1664]{2,1,0:T(8,128)(2,1)}) fusion(f32[49,1664]{1,0:T(8,128)S(1)} %get-tuple-element.7, f32[16,1664]{1,0:T(8,128)S(1)} %get-tuple-element.5, f32[49,1664]{1,0:T(8,128)S(1)} %get-tuple-element.6, f32[16,1664]{1,0:T(8,128)S(1)} %get-tuple-element.4), kind=kLoop, calls=%fused_computation | loop fusion | flops 10436608 | bytes 6083584 | tf_op jit(solution)/shard_map/convert.3
  12.9 3.3 %sub.60 = bf16[784,1664]{1,0:T(8,128)(2,1)} reshape(bf16[16,49,1664]{2,1,0:T(8,128)(2,1)} %get-tuple-element.3) | data formatting | bytes 5218304 | tf_op jit(solution)/shard_map/sub | solution.py:31
  16.2 3.5 %constant_dynamic-update-slice_fusion.1 = bf16[784,3328]{1,0:T(8,128)(2,1)} fusion(bf16[784,1664]{1,0:T(8,128)(2,1)} %sub.60), kind=kLoop, calls=%fused_computation.36 | loop fusion | bytes 5218304
  19.7 1.9 %add.100 = bf16[784,1664]{1,0:T(8,128)(2,1)} reshape(bf16[16,49,1664]{2,1,0:T(8,128)(2,1)S(1)} %get-tuple-element.2) | data formatting | bytes 5218304 | tf_op jit(solution)/shard_map/add | solution.py:32
  21.6 16.3 %all_gather.3 = bf16[1,32,3328]{2,0,1:T(2,128)(2,1)S(1)} all-gather(bf16[1,4,3328]{2,0,1:T(2,128)(2,1)S(1)} %copy.10), channel_id=1, replica_groups=mesh['band'=4,'img'=8] {'img'}, dimensions={1}, use_global_device_ids=true | all-gather | bytes 239616 | tf_op jit(solution)/shard_map/all_gather | solution.py:85
  38.0 0.4 convert_element_type.42
  38.5 0.2 fusion.3
  38.7 0.1 reshape.205
  38.9 3.5 %constant_dynamic-update-slice_fusion = bf16[784,3328]{1,0:T(8,128)(2,1)} fusion(bf16[784,3328]{1,0:T(8,128)(2,1)} %constant_dynamic-update-slice_fusion.1, bf16[784,1664]{1,0:T(8,128)(2,1)} %add.100), kind=kLoop, calls=%fused_computation.35 | loop fusion | bytes 5218304 | tf_op jit(solution)/shard_map/concatenate | solution.py:33
  42.3 4.8 %fusion = f32[784,32]{0,1:T(8,128)} fusion(f32[784,32]{0,1:T(8,128)S(1)} %reshape.205, bf16[784,3328]{1,0:T(8,128)(2,1)} %constant_dynamic-update-slice_fusion, f32[1,32,3328]{2,0,1:T(1,128)S(1)} %convert_element_type.42, f32[3328]{0:T(1024)S(1)} %pad_maximum_fusion, f32[32]{0:T(128)S(1)} %broadcast_multiply_fusion), kind=kOutput, calls=%fused_computation.3 | convolution fusion | flops 167248896 | bytes 5858432 | tf_op jit(solution)/shard_map/dot_general | solution.py:56
  47.2 42.6 %all-reduce.5.cloned.1.call-done = f32[784,32]{0,1:T(8,128)} async-done(((f32[784,32]{0,1:T(8,128)}), f32[784,32]{0,1:T(8,128)}) %all-reduce.5.cloned.1.call-update) | async-done | bytes 100368 | tf_op jit(solution)/shard_map/psum | solution.py:70
  89.8 1.0 reduce_max.10
  90.9 0.1 reduce_max.18
  91.2 0.9 fusion.9
  92.2 0.1 reduce_sum.37
  92.5 4.3 %fusion.10 = f32[32,3328]{1,0:T(8,128)} fusion(bf16[784,3328]{1,0:T(8,128)(2,1)} %constant_dynamic-update-slice_fusion, f32[784,32]{0,1:T(8,128)} %all-reduce.5.cloned.1.call-done, f32[784]{0:T(1024)S(1)} %div.25, f32[784]{0:T(1024)S(1)} %sub.67), kind=kOutput, calls=%fused_computation.16 | convolution fusion | flops 167060992 | bytes 5750912 | tf_op jit(solution)/shard_map/dot_general | solution.py:91
  96.8 0.6 dynamic-slice
  98.0 0.1 fusion.12
  98.2 16.0 %all-reduce.1 = f32[32]{0:T(128)S(1)} all-reduce(f32[32]{0:T(128)S(1)} %fusion.12), channel_id=3, replica_groups=mesh['band'=4,'img'=8] {'img'}, use_global_device_ids=true, to_apply=%region_8.9.clone | all-reduce | flops 32 | bytes 256
  114.2 0.6 dynamic-slice.3
  114.8 37.6 %all-reduce.7.cloned.1.call-done = f32[32,3328]{1,0:T(8,128)} async-done(((f32[32,3328]{1,0:T(8,128)}), f32[32,3328]{1,0:T(8,128)}) %all-reduce.7.cloned.1.call-update) | async-done | bytes 426000
  152.4 1.5 dynamic-slice_bitcast_fusion
  (29 shorter events, 0.8 us)
Async XLA Ops:
  7.2 82.7 %all-reduce.5.cloned.1.call-start = ((), (), s32[]{:S(2)}) async-start(), calls=%async_computation | async-start | bytes 229376 | tf_op jit(solution)/shard_map/psum | solution.py:70
  16.2 5.4 %copy-start.1 = (bf16[1,4,3328]{2,1,0:T(4,128)(2,1)S(1)}, bf16[1,4,3328]{2,1,0:T(4,128)(2,1)}, u32[]{:S(2)}) copy-start(bf16[1,4,3328]{2,1,0:T(4,128)(2,1)} %param.5) | copy-start | bytes 79876
  16.2 22.2 %copy-start.3 = (f32[1,1664]{1,0:T(1,128)S(1)}, f32[1,1664]{1,0:T(1,128)}, u32[]{:S(2)}) copy-start(f32[1,1664]{1,0:T(1,128)} %param.6) | copy-start | bytes 19972
  16.2 22.5 %copy-start.2 = (s32[1,2,8,49]{3,2,1,0:T(8,128)S(1)}, s32[1,2,8,49]{3,2,1,0:T(8,128)}, u32[]{:S(2)}) copy-start(s32[1,2,8,49]{3,2,1,0:T(8,128)} %param.7) | copy-start | bytes 9412
  47.1 49.7 %copy-start.4 = (u32[32]{0:T(128)S(1)}, u32[32]{0:T(128)}, u32[]{:S(2)}) copy-start(u32[32]{0:T(128)} %constant.76) | copy-start | bytes 388
  47.1 105.3 %all-reduce.7.cloned.1.call-start = ((), (), s32[]{:S(2)}) async-start(), calls=%async_computation.1 | async-start | bytes 851968
  89.8 8.2 %copy-start = (f32[784,32]{0,1:T(8,128)S(1)}, f32[784,32]{0,1:T(8,128)}, u32[]{:S(2)}) copy-start(f32[784,32]{0,1:T(8,128)} %all-reduce.5.cloned.1.call-done) | copy-start | bytes 301060
Sparse Core Ops, SparseCore 0:
  47.2 42.5 all-reduce.4
  96.9 55.4 all-reduce.6
where the time goes:
time: 161 us
  waiting for transfers between devices  80.3 us (50%)
  blocking collectives  32.4 us (20%)
  local copies, waits for them, and re-layouts  15.6 us (10%)
  between operations  14.8 us (9%)
  matrix products  9.05 us (6%)
  other arithmetic  8.56 us (5%)
    psum x1, waiting for transfers between devices, combine_bands(): total = lax.psum(partial_score, 'band')  42.6 us
    unnamed x3, waiting for transfers between devices  37.7 us
    all_gather x1, blocking collectives, per_device(): lax.all_gather(references, 'img', axis=1, tiled=True)[0]  16.3 us
    unnamed x1, blocking collectives  16 us
    dot_general x1, matrix products, band_term(): lax.dot_general(aligned, weighted, (((1,), (1,)), ((), ())), preferred_el...  4.78 us
    unnamed x14, local copies, waits for them, and re-layouts  4.7 us
    dot_general x1, matrix products, per_device(): lax.dot_general(post, aligned, (((0,), (0,)), ((), ())), preferred_elemen...  4.28 us
    concatenate x1, local copies, waits for them, and re-layouts, align(): joined = jnp.concatenate([out_real, out_imag], axis=2).astype(jnp.bfloat16)  3.46 us
  transfers between devices with their start and end apart: 2, of which 2 were waited for; matrix products, arithmetic and copies ran while one was open for 1% of the time, Pallas kernels for 0%

commit v1 on v0

--- a/solution.py
+++ b/solution.py
@@ -67,7 +67,7 @@
 
 
 def combine_bands(partial_score):
-    total = lax.psum(partial_score, "band")
+    total = jnp.sum(lax.all_gather(partial_score, "band"), axis=0)
     return total
 
 

time: 161 us -> 125 us (0.78)
  waiting for transfers between devices: 80.3 us -> 38 us
  blocking collectives: 32.4 us -> 41.1 us
  other arithmetic: 8.56 us -> 6.72 us
    psum x1 -> x0, waiting for transfers between devices: 42.6 us -> none  [combine_bands(): total = lax.psum(partial_score, 'band')]
    all_gather x0 -> x1, blocking collectives: none -> 9.78 us  [combine_bands(): total = jnp.sum(lax.all_gather(partial_score, 'band'), axis=0)]
    unnamed x3 -> x2, waiting for transfers between devices: 37.7 us -> 38 us
    unnamed x14 -> x12, local copies, waits for them, and re-layouts: 4.7 us -> 4.71 us
  transfers between devices with their start and end apart: 2 -> 1, of which waited for: 2 -> 1; matrix products, arithmetic and copies ran while one was open for 1% -> 1% of each run, Pallas kernels for 0% -> 0%
where the time goes in v1:
time: 125 us
  blocking collectives  41.1 us (33%)
  waiting for transfers between devices  38 us (30%)
  local copies, waits for them, and re-layouts  15.6 us (12%)
  between operations  14.8 us (12%)
  matrix products  8.3 us (7%)
  other arithmetic  6.72 us (5%)
    unnamed x2, waiting for transfers between devices  38 us
    all_gather x1, blocking collectives, per_device(): lax.all_gather(references, 'img', axis=1, tiled=True)[0]  16.3 us
    unnamed x1, blocking collectives  15 us
    all_gather x1, blocking collectives, combine_bands(): total = jnp.sum(lax.all_gather(partial_score, 'band'), axis=0)  9.78 us
    unnamed x12, local copies, waits for them, and re-layouts  4.71 us
    dot_general x1, matrix products, per_device(): lax.dot_general(post, aligned, (((0,), (0,)), ((), ())), preferred_elemen...  4.21 us
    dot_general x1, matrix products, band_term(): lax.dot_general(aligned, weighted, (((1,), (1,)), ((), ())), preferred_el...  4.09 us
    concatenate x1, local copies, waits for them, and re-layouts, align(): joined = jnp.concatenate([out_real, out_imag], axis=2).astype(jnp.bfloat16)  3.46 us
  transfers between devices with their start and end apart: 1, of which 1 were waited for; matrix products, arithmetic and copies ran while one was open for 1% of the time, Pallas kernels for 0%

profile of v1, /device:TPU:0, one launch (start us, length us, event | category | flops | bytes accessed | tf_op | source)
XLA Modules:
  0.0 124.6 jit_solution(2022825206333499582)
XLA Ops:
  7.2 0.9 slice_convert_fusion.1
  8.1 1.4 %fusion.6 = (f32[49,1664]{1,0:T(8,128)S(1)}, f32[49,1664]{1,0:T(8,128)S(1)}) fusion(s32[1664]{0:T(1024)S(1)} %get-tuple-element.8, s32[49]{0:T(128)S(1)} %get-tuple-element.10, s32[1664]{0:T(1024)S(1)} %get-tuple-element.9, s32[49]{0:T(128)S(1)} %get-tuple-element.11), kind=kLoop, calls=%fused_computation.12 | loop fusion | flops 407680 | bytes 665992 | tf_op jit(solution)/shard_map/cos | solution.py:24
  9.5 3.3 %add_convert_fusion = (bf16[16,49,1664]{2,1,0:T(8,128)(2,1)S(1)}, bf16[16,49,1664]{2,1,0:T(8,128)(2,1)}) fusion(f32[49,1664]{1,0:T(8,128)S(1)} %get-tuple-element.7, f32[16,1664]{1,0:T(8,128)S(1)} %get-tuple-element.5, f32[49,1664]{1,0:T(8,128)S(1)} %get-tuple-element.6, f32[16,1664]{1,0:T(8,128)S(1)} %get-tuple-element.4), kind=kLoop, calls=%fused_computation | loop fusion | flops 10436608 | bytes 6083584 | tf_op jit(solution)/shard_map/convert.3
  12.9 3.3 %sub.60 = bf16[784,1664]{1,0:T(8,128)(2,1)} reshape(bf16[16,49,1664]{2,1,0:T(8,128)(2,1)} %get-tuple-element.3) | data formatting | bytes 5218304 | tf_op jit(solution)/shard_map/sub | solution.py:31
  16.2 3.5 %constant_dynamic-update-slice_fusion.1 = bf16[784,3328]{1,0:T(8,128)(2,1)} fusion(bf16[784,1664]{1,0:T(8,128)(2,1)} %sub.60), kind=kLoop, calls=%fused_computation.37 | loop fusion | bytes 5218304
  19.7 1.9 %add.98 = bf16[784,1664]{1,0:T(8,128)(2,1)} reshape(bf16[16,49,1664]{2,1,0:T(8,128)(2,1)S(1)} %get-tuple-element.2) | data formatting | bytes 5218304 | tf_op jit(solution)/shard_map/add | solution.py:32
  21.6 16.3 %all_gather.9 = bf16[1,32,3328]{2,0,1:T(2,128)(2,1)S(1)} all-gather(bf16[1,4,3328]{2,0,1:T(2,128)(2,1)S(1)} %copy.10), channel_id=1, replica_groups=mesh['band'=4,'img'=8] {'img'}, dimensions={1}, use_global_device_ids=true | all-gather | bytes 239616 | tf_op jit(solution)/shard_map/all_gather | solution.py:85
  38.0 0.4 convert_element_type.42
  38.5 0.2 fusion.4
  38.7 0.1 reshape.205
  38.9 3.5 %constant_dynamic-update-slice_fusion = bf16[784,3328]{1,0:T(8,128)(2,1)} fusion(bf16[784,3328]{1,0:T(8,128)(2,1)} %constant_dynamic-update-slice_fusion.1, bf16[784,1664]{1,0:T(8,128)(2,1)} %add.98), kind=kLoop, calls=%fused_computation.36 | loop fusion | bytes 5218304 | tf_op jit(solution)/shard_map/concatenate | solution.py:33
  42.3 4.1 %fusion.1 = f32[1,784,32]{1,2,0:T(8,128)S(1)} fusion(f32[784,32]{0,1:T(8,128)S(1)} %reshape.205, bf16[784,3328]{1,0:T(8,128)(2,1)} %constant_dynamic-update-slice_fusion, f32[1,32,3328]{2,0,1:T(1,128)S(1)} %convert_element_type.42, f32[3328]{0:T(1024)S(1)} %pad_maximum_fusion, f32[32]{0:T(128)S(1)} %broadcast_multiply_fusion), kind=kOutput, calls=%fused_computation.4 | convolution fusion | flops 167248896 | bytes 5858432 | tf_op jit(solution)/shard_map/dot_general | solution.py:56
  46.4 9.8 %all-gather.1 = f32[4,784,32]{1,2,0:T(8,128)S(1)} all-gather(f32[1,784,32]{1,2,0:T(8,128)S(1)} %fusion.1), channel_id=2, replica_groups=mesh['band'=4,'img'=8] {'band'}, dimensions={0}, use_global_device_ids=true | all-gather | bytes 501760 | tf_op jit(solution)/shard_map/all_gather | solution.py:70
  56.4 0.1 reduce_max.18
  56.5 0.1 sub.67
  56.8 0.1 reduce_sum.47
  57.0 0.1 div.25
  57.1 4.2 %fusion.11 = f32[32,3328]{1,0:T(8,128)} fusion(bf16[784,3328]{1,0:T(8,128)(2,1)} %constant_dynamic-update-slice_fusion, f32[784,32]{0,1:T(8,128)S(1)} %reduce_sum.44, f32[784]{0:T(1024)S(1)} %div.25, f32[784]{0:T(1024)S(1)} %sub.67), kind=kOutput, calls=%fused_computation.17 | convolution fusion | flops 167060992 | bytes 5750912 | tf_op jit(solution)/shard_map/dot_general | solution.py:91
  61.3 0.6 dynamic-slice
  62.5 0.1 fusion.13
  62.7 15.0 %all-reduce.1 = f32[32]{0:T(128)S(1)} all-reduce(f32[32]{0:T(128)S(1)} %fusion.13), channel_id=4, replica_groups=mesh['band'=4,'img'=8] {'img'}, use_global_device_ids=true, to_apply=%region_8.9.clone | all-reduce | flops 32 | bytes 256
  77.6 0.6 dynamic-slice.3
  78.2 38.0 %all-reduce.4.cloned.1.call-done = f32[32,3328]{1,0:T(8,128)} async-done(((f32[32,3328]{1,0:T(8,128)}), f32[32,3328]{1,0:T(8,128)}) %all-reduce.4.cloned.1.call-update) | async-done | bytes 426000
  116.3 1.5 %dynamic-slice_bitcast_fusion = f32[1,4,3328]{2,1,0:T(4,128)} fusion(f32[32,3328]{1,0:T(8,128)} %all-reduce.4.cloned.1.call-done, u32[]{:T(128)S(6)} %multiply.1), kind=kLoop, calls=%fused_computation.21 | loop fusion | bytes 106500 | tf_op jit(solution)/shard_map/broadcast_in_dim | solution.py:98
  (26 shorter events, 0.6 us)
Async XLA Ops:
  7.2 109.1 %all-reduce.4.cloned.1.call-start = ((), (), s32[]{:S(2)}) async-start(), calls=%async_computation | async-start | bytes 851968
  16.2 5.4 %copy-start = (bf16[1,4,3328]{2,1,0:T(4,128)(2,1)S(1)}, bf16[1,4,3328]{2,1,0:T(4,128)(2,1)}, u32[]{:S(2)}) copy-start(bf16[1,4,3328]{2,1,0:T(4,128)(2,1)} %param.5) | copy-start | bytes 79876
  16.2 22.2 %copy-start.2 = (f32[1,1664]{1,0:T(1,128)S(1)}, f32[1,1664]{1,0:T(1,128)}, u32[]{:S(2)}) copy-start(f32[1,1664]{1,0:T(1,128)} %param.6) | copy-start | bytes 19972
  16.2 22.5 %copy-start.1 = (s32[1,2,8,49]{3,2,1,0:T(8,128)S(1)}, s32[1,2,8,49]{3,2,1,0:T(8,128)}, u32[]{:S(2)}) copy-start(s32[1,2,8,49]{3,2,1,0:T(8,128)} %param.7) | copy-start | bytes 9412
  46.4 14.9 %copy-start.3 = (u32[32]{0:T(128)S(1)}, u32[32]{0:T(128)}, u32[]{:S(2)}) copy-start(u32[32]{0:T(128)} %constant.76) | copy-start | bytes 388
Sparse Core Ops, SparseCore 0:
  61.4 54.8 all-reduce.3
